TPU v7x, 512 devices: a whole 4x4x16 slice. The times are simulated.
512 devices in a mesh: flux: 16 (over z), obs: 32 (over y, x, core).
Axes of the slice: x: 4, y: 4, z: 16, core: 2. Of those that a mesh axis runs over, the one named last changes fastest.
Arguments:
- footprint: bfloat16 [4096, 4, 4, 2, 4096], P(('flux', 'obs')), may hold values from 0.00049972534 to 0.049804688
- obs_hour: int32 [4096, 4], P(('flux', 'obs')), may hold values from 0 to 3
- tile_list: int32 [4096, 4], P(('flux', 'obs')), may hold values from 0 to 511, as said below
- tile_row: int32 [512], replicated, may hold values from 0 to 511, as said below
- flux: bfloat16 [512, 5, 4096], P('flux'), may hold values from -6 to 6
- observed: float32 [4096, 4], P(('flux', 'obs')), may hold values from -18 to 18
- obs_var: float32 [4096, 4], P(('flux', 'obs')), may hold values from 0.5 to 4
Outputs:
- modeled: float32 [4096, 4], P(('flux', 'obs'))
- gradient: float32 [512, 5, 4096], P('flux', None, 'obs')
Inputs may be any that keep to these rules, and one draw needn't show every extreme that they name: `tile_row`: A permutation: every tile has its own storage row, and the row r lies on index r // 32 of flux. `tile_list`: among the 32 listed tiles of one device's 8 blocks, at most 4 have storage rows on one index of flux; on every device some index of flux gets exactly 4.
All inputs are finite; a program needn't handle non-finite values.
Results may differ from a plain program's by a relative error of at most 0.0019.
Values may be sent and summed in bfloat16 or wider, within the bound.
A program may use at most 64 MiB of HBM per device.

v0:
```python
import jax
import jax.numpy as jnp
from jax import lax
from jax.sharding import PartitionSpec as P


def shards(footprint, obs_hour, tile_list, tile_row, flux, observed, obs_var):
    columns = lax.axis_size("obs")
    block_count, slot_width, sounding_count, lag_count, cell_count = footprint.shape
    tile_count, hour_count, _ = flux.shape
    chunk = cell_count // columns
    me = lax.axis_index("obs")
    table_hits = tile_list[..., None] == jnp.arange(tile_row.shape[0], dtype=jnp.int32)
    storage = jnp.sum(jnp.where(table_hits, tile_row, 0), axis=-1)
    numbers = jnp.concatenate(
        [storage.astype(jnp.float32), obs_hour.astype(jnp.float32), observed, obs_var], axis=1
    )
    numbers = lax.all_gather(numbers, "obs", axis=0, tiled=True)
    rows = numbers[:, 0:4].astype(jnp.int32)
    hours = numbers[:, 4:8].astype(jnp.int32)
    own_flux = lax.dynamic_slice_in_dim(flux, me * chunk, chunk, axis=2)
    all_flux = lax.all_gather(own_flux, "flux", axis=0, tiled=True)
    total = all_flux.shape[0]
    feet = footprint.reshape(-1, columns, chunk).transpose(1, 0, 2)
    feet = lax.all_to_all(feet, "obs", split_axis=0, concat_axis=0, tiled=True)
    blocks = block_count * columns
    feet = feet.reshape(blocks, slot_width, sounding_count, lag_count, chunk)
    onehot = rows.reshape(-1)[:, None] == jnp.arange(total, dtype=jnp.int32)[None, :]
    windows = jnp.dot(
        onehot.astype(jnp.bfloat16),
        all_flux.reshape(total, hour_count * chunk),
        preferred_element_type=jnp.float32,
    ).reshape(blocks, slot_width, hour_count, chunk)
    hour_at = hours[:, :, None] + jnp.arange(lag_count, dtype=jnp.int32)
    select = hour_at[..., None] == jnp.arange(hour_count, dtype=jnp.int32)
    picked = 0.0
    for h in range(hour_count):
        picked = picked + jnp.where(
            select[:, None, :, :, h, None], windows[:, :, None, None, h, :], 0.0
        )
    partial_value = jnp.sum(feet.astype(jnp.float32) * picked, axis=(1, 3, 4))
    modeled_all = lax.psum(partial_value, "obs")
    scaled = ((modeled_all - numbers[:, 8:12]) / numbers[:, 12:16]).astype(jnp.bfloat16)
    modeled = lax.dynamic_slice_in_dim(modeled_all, me * block_count, block_count, axis=0)
    coefficient = jnp.where(select, scaled.astype(jnp.float32)[:, :, None, None], 0.0)
    terms = []
    for h in range(hour_count):
        terms.append(
            jnp.sum(feet.astype(jnp.float32) * coefficient[:, None, :, :, h, None], axis=(2, 3))
        )
    terms = jnp.stack(terms, axis=2).reshape(blocks * slot_width, hour_count * chunk)
    high = terms.astype(jnp.bfloat16)
    low = (terms - high.astype(jnp.float32)).astype(jnp.bfloat16)
    spread = onehot.astype(jnp.bfloat16)
    summed = lax.dot_general(
        spread, high, (((0,), (0,)), ((), ())), preferred_element_type=jnp.float32
    ) + lax.dot_general(spread, low, (((0,), (0,)), ((), ())), preferred_element_type=jnp.float32)
    gradient = lax.psum_scatter(
        summed.reshape(total, hour_count, chunk), "flux", scatter_dimension=0, tiled=True
    )
    return (modeled, gradient)


def solution(mesh):
    placed = (
        P(("flux", "obs"), None, None, None, None),
        P(("flux", "obs"), None),
        P(("flux", "obs"), None),
        P(),
        P("flux", None, None),
        P(("flux", "obs"), None),
        P(("flux", "obs"), None),
    )
    return jax.shard_map(
        shards,
        mesh=mesh,
        in_specs=placed,
        out_specs=(P(("flux", "obs"), None), P("flux", None, "obs")),
        check_vma=False,
    )
```

profile of v0, /device:TPU:8, one launch (start us, length us, event | category | flops | bytes accessed | tf_op | source)
XLA Modules:
  0.0 355.8 jit_solution(15153389452616925642)
XLA Ops:
  7.2 3.4 reshape.75
  10.7 2.2 copy.126
  12.8 9.5 %all-to-all-start = ((bf16[32,256,128]{2,1,0:T(8,128)(2,1)}), bf16[32,256,128]{2,1,0:T(8,128)(2,1)S(1)}, u32[]{:S(2)}, u32[]{:S(2)}) async-start(bf16[32,256,128]{2,1,0:T(8,128)(2,1)} %copy.126), calls=%async_computation | async-start | bytes 4194304 | tf_op jit(solution)/shard_map/all_to_all | solution.py:25
  22.8 42.4 %all_gather.6 = f32[256,16]{1,0:T(8,128)S(1)} all-gather(f32[8,16]{1,0:T(8,128)S(1)} %copy.127), channel_id=1, replica_groups=mesh['flux'=16,'obs'=32] {'obs'}, dimensions={0}, use_global_device_ids=true | all-gather | bytes 16896 | tf_op jit(solution)/shard_map/all_gather | solution.py:18
  67.5 1.6 copy.157
  70.1 1.6 copy.158
  73.2 1.6 copy.139
  74.8 1.6 copy.137
  78.3 2.0 broadcast_in_dim.153
  80.3 2.6 broadcast_in_dim.154
  82.9 2.0 broadcast_in_dim.160
  85.0 3.2 broadcast_in_dim.161
  88.2 2.0 broadcast_in_dim.167
  90.2 3.2 broadcast_in_dim.168
  93.5 2.0 broadcast_in_dim.174
  95.5 3.2 broadcast_in_dim.175
  98.7 1.1 broadcast_in_dim.145
  99.9 2.6 broadcast_in_dim.146
  102.5 39.7 %all_gather.7 = bf16[512,5,128]{2,0,1:T(8,128)(2,1)} all-gather(bf16[32,5,128]{2,0,1:T(8,128)(2,1)S(1)} %constant_dynamic-slice_fusion), channel_id=1, replica_groups=mesh['flux'=16,'obs'=32] {'flux'}, dimensions={0}, use_global_device_ids=true | all-gather | bytes 696320 | tf_op jit(solution)/shard_map/all_gather | solution.py:22
  142.3 2.2 copy.131
  144.4 2.2 fusion.4
  146.8 1.1 copy.132
  148.0 1.1 copy.140
  149.1 1.1 copy.138
  150.3 1.2 copy.136
  151.4 1.1 copy.134
  152.5 2.2 broadcast_in_dim.157
  154.8 1.1 broadcast_in_dim.164
  155.9 1.1 broadcast_in_dim.171
  157.0 1.1 broadcast_in_dim.178
  158.1 1.1 broadcast_in_dim.149
  159.2 8.6 %multiply_reduce_fusion.5 = f32[32,256]{1,0:T(8,128)S(1)} fusion(f32[32,256,128]{2,1,0:T(8,128)S(1)} %bitcast.76, f32[32,256,128]{2,1,0:T(8,128)S(1)} %bitcast.75, f32[32,256,128]{2,1,0:T(8,128)S(1)} %bitcast.74, f32[32,256,128]{2,1,0:T(8,128)S(1)} %bitcast.73, f32[32,256,128]{2,1,0:T(8,128)S(1)} %bitcast.77, pred[32,256]{1,0:T(8,128)(4,1)S(1)} %copy-done.7, ...), kind=kLoop, calls=%fused_computation.5 | loop fusion | flops 12574720 | bytes 23142400 | tf_op jit(solution)/shard_map/reduce_sum | solution.py:41
  167.8 4.0 %reduce_sum.72 = f32[256,4,4,2]{3,2,1,0:T(4,128)} reshape(f32[32,256]{1,0:T(8,128)S(1)} %multiply_reduce_fusion.5) | data formatting | bytes 65536 | tf_op jit(solution)/shard_map/reduce_sum | solution.py:41
  171.9 2.1 reduce_sum.73
  174.0 53.2 %psum.7 = f32[256,4]{0,1:T(4,128)S(1)} all-reduce(f32[256,4]{0,1:T(4,128)S(1)} %copy.143), channel_id=1, replica_groups=mesh['flux'=16,'obs'=32] {'obs'}, use_global_device_ids=true, to_apply=%region_3.4 | all-reduce | flops 1024 | bytes 8192 | tf_op jit(solution)/shard_map/psum | solution.py:42
  228.0 1.0 copy.146
  229.0 1.0 copy.150
  230.0 1.0 copy.149
  231.1 1.0 copy.148
  232.1 1.0 copy.147
  233.2 18.6 %multiply_reduce_fusion = (f32[256,4,128]{2,1,0:T(4,128)}, f32[256,4,128]{2,1,0:T(4,128)}, f32[256,4,128]{2,1,0:T(4,128)}, f32[256,4,128]{2,1,0:T(4,128)}, f32[256,4,128]{2,1,0:T(4,128)}) fusion(f32[256,4,2]{2,1,0:T(4,128)} %copy.150, f32[256,4,2]{2,1,0:T(4,128)} %copy.149, f32[256,4,2]{2,1,0:T(4,128)} %copy.148, f32[256,4,2]{2,1,0:T(4,128)} %copy.147, ...), kind=kLoop, calls=%fused_computation | loop fusion | flops 10878976 | bytes 4759552 | tf_op jit(solution)/shard_map/reduce_sum | solution.py:49
  251.8 10.5 %stack.23 = f32[256,4,5,128]{3,2,1,0:T(8,128)} concatenate(f32[256,4,1,128]{3,2,1,0:T(1,128)} %bitcast.86, f32[256,4,1,128]{3,2,1,0:T(1,128)} %bitcast.85, f32[256,4,1,128]{3,2,1,0:T(1,128)} %bitcast.84, f32[256,4,1,128]{3,2,1,0:T(1,128)} %bitcast.83, f32[256,4,1,128]{3,2,1,0:T(1,128)} %bitcast.82), dimensions={2} | concatenate | bytes 5242880 | tf_op jit(solution)/shard_map/stack | solution.py:51
  262.3 3.5 fusion.1
  265.8 4.4 %fusion.6 = f32[512,640]{1,0:T(8,128)} fusion(f32[512,640]{1,0:T(8,128)S(1)} %fusion.1, f32[128,8,5,128]{3,2,1,0:T(8,128)} %bitcast.81, s32[1024]{0:T(1024)S(1)} %copy-done.9), kind=kOutput, calls=%fused_computation.15 | convolution fusion | flops 671940608 | bytes 5246976 | tf_op jit(solution)/shard_map/dot_general | solution.py:55
  270.2 1.7 copy.151
  271.9 1.8 copy.152
  274.4 72.9 %reduce-scatter.2.cloned.1.call-done = f32[32,5,128]{2,1,0:T(8,128)} async-done(((f32[512,5,128]{2,1,0:T(8,128)}), f32[32,5,128]{2,1,0:T(8,128)}) %reduce-scatter.2.cloned.1.call-update) | async-done | bytes 81936 | tf_op jit(solution)/shard_map/reduce_scatter | solution.py:58
  347.4 1.6 copy.153
  (56 shorter events, 8.8 us)
Async XLA Ops:
  7.2 95.3 %copy-start = (bf16[32,5,4096]{2,0,1:T(8,128)(2,1)S(1)}, bf16[32,5,4096]{2,0,1:T(8,128)(2,1)}, u32[]{:S(2)}) copy-start(bf16[32,5,4096]{2,0,1:T(8,128)(2,1)} %param.11) | copy-start | bytes 3932164
  10.6 11.8 %copy-start.12 = (s32[8,4]{0,1:T(4,128)S(1)}, s32[8,4]{0,1:T(4,128)}, u32[]{:S(2)}) copy-start(s32[8,4]{0,1:T(4,128)} %param.8) | copy-start | bytes 388
  10.6 11.8 %copy-start.10 = (s32[512]{0:T(512)S(1)}, s32[512]{0:T(512)}, u32[]{:S(2)}) copy-start(s32[512]{0:T(512)} %param.10) | copy-start | bytes 6148
  10.6 11.8 %copy-start.11 = (s32[8,4]{0,1:T(4,128)S(1)}, s32[8,4]{0,1:T(4,128)}, u32[]{:S(2)}) copy-start(s32[8,4]{0,1:T(4,128)} %param.9) | copy-start | bytes 388
  10.7 12.1 %copy-start.13 = (f32[8,4]{0,1:T(4,128)S(1)}, f32[8,4]{0,1:T(4,128)}, u32[]{:S(2)}) copy-start(f32[8,4]{0,1:T(4,128)} %param.13) | copy-start | bytes 388
  10.7 12.1 %copy-start.14 = (f32[8,4]{0,1:T(4,128)S(1)}, f32[8,4]{0,1:T(4,128)}, u32[]{:S(2)}) copy-start(f32[8,4]{0,1:T(4,128)} %param.12) | copy-start | bytes 388
  12.8 139.7 %all-to-all-start = ((bf16[32,256,128]{2,1,0:T(8,128)(2,1)}), bf16[32,256,128]{2,1,0:T(8,128)(2,1)S(1)}, u32[]{:S(2)}, u32[]{:S(2)}) async-start(bf16[32,256,128]{2,1,0:T(8,128)(2,1)} %copy.126), calls=%async_computation | async-start | bytes 4194304 | tf_op jit(solution)/shard_map/all_to_all | solution.py:25
  22.4 325.0 %reduce-scatter.2.cloned.1.call-start = ((), (), s32[]{:S(2)}) async-start(), calls=%async_computation.2 | async-start | bytes 2228224 | tf_op jit(solution)/shard_map/reduce_scatter | solution.py:58
  152.5 2.2 copy-start.4
  152.5 3.3 copy-start.3
  154.8 2.2 copy-start.2
  155.9 2.2 copy-start.1
  157.0 2.2 copy-start.5
  157.0 2.2 copy-start.6
  157.0 2.2 copy-start.7
  167.8 59.4 %copy-start.8 = (f32[256,4]{0,1:T(4,128)S(1)}, f32[256,4]{0,1:T(4,128)}, u32[]{:S(2)}) copy-start(f32[256,4]{0,1:T(4,128)} %copy.157) | copy-start | bytes 12292
  251.8 10.5 %copy-start.9 = (s32[1024]{0:T(1024)S(1)}, s32[1024]{0:T(1024)}, u32[]{:S(2)}) copy-start(s32[1024]{0:T(1024)} %eq.73) | copy-start | bytes 12292
Sparse Core Ops, SparseCore 0:
  273.9 73.4 reduce-scatter.1
where the time goes:
time: 358 us; the launch traced here: 356 us
  blocking collectives  135 us (38%)
  local copies, waits for them, and re-layouts  82.3 us (23%)
  waiting for transfers between devices  72.9 us (20%)
  other arithmetic  31.1 us (9%)
  between operations  14.4 us (4%)
  matrix products  10.1 us (3%)
  starting transfers between devices  9.58 us (3%)
    reduce_scatter x1, waiting for transfers between devices, shards(): lax.psum_scatter(summed.reshape(total, hour_count, chunk), 'flux', scatte...  72.9 us
    psum x1, blocking collectives, shards(): modeled_all = lax.psum(partial_value, 'obs')  53.2 us
    broadcast_in_dim x27, local copies, waits for them, and re-layouts, shards(): jnp.where(select[:, None, :, :, h, None], windows[:, :, None, None, h, :]...  43.3 us
    all_gather x1, blocking collectives, shards(): numbers = lax.all_gather(numbers, 'obs', axis=0, tiled=True)  42.4 us
    all_gather x1, blocking collectives, shards(): all_flux = lax.all_gather(own_flux, 'flux', axis=0, tiled=True)  39.7 us
    reduce_sum x1, other arithmetic, shards(): jnp.sum(feet.astype(jnp.float32) * coefficient[:, None, :, :, h, None], a...  18.6 us
    reduce_sum x2, other arithmetic, shards(): partial_value = jnp.sum(feet.astype(jnp.float32) * picked, axis=(1, 3, 4))  10.7 us
    another operation x1, local copies, waits for them, and re-layouts, shards(): jnp.stack(terms, axis=2).reshape(blocks * slot_width, hour_count * chunk)  10.5 us
  transfers between devices with their start and end apart: 2, of which 1 were waited for; matrix products, arithmetic and copies ran while one was open for 14% of the time, Pallas kernels for 0%

commit v1 on v0

--- a/solution.py
+++ b/solution.py
@@ -39,7 +39,11 @@
             select[:, None, :, :, h, None], windows[:, :, None, None, h, :], 0.0
         )
     partial_value = jnp.sum(feet.astype(jnp.float32) * picked, axis=(1, 3, 4))
-    modeled_all = lax.psum(partial_value, "obs")
+    modeled_all = partial_value
+    for hop in (1, 2, 4, 8, 16):
+        modeled_all = modeled_all + lax.ppermute(
+            modeled_all, "obs", [(dev, dev ^ hop) for dev in range(32)]
+        )
     scaled = ((modeled_all - numbers[:, 8:12]) / numbers[:, 12:16]).astype(jnp.bfloat16)
     modeled = lax.dynamic_slice_in_dim(modeled_all, me * block_count, block_count, axis=0)
     coefficient = jnp.where(select, scaled.astype(jnp.float32)[:, :, None, None], 0.0)

time: 358 us -> 338 us (0.944)
  the two profiles are of different devices: /device:TPU:8 before, /device:TPU:2 now
where the time goes in v1:
time: 338 us; the launch traced here: 336 us
  local copies, waits for them, and re-layouts  84.7 us (25%)
  waiting for transfers between devices  83.4 us (25%)
  blocking collectives  80.8 us (24%)
  other arithmetic  35 us (10%)
  starting transfers between devices  27.2 us (8%)
  between operations  14.4 us (4%)
  matrix products  10.1 us (3%)
    reduce_scatter x1, waiting for transfers between devices, shards(): lax.psum_scatter(summed.reshape(total, hour_count, chunk), 'flux', scatte...  67.2 us
    broadcast_in_dim x27, local copies, waits for them, and re-layouts, shards(): jnp.where(select[:, None, :, :, h, None], windows[:, :, None, None, h, :]...  45.4 us
    all_gather x1, blocking collectives, shards(): numbers = lax.all_gather(numbers, 'obs', axis=0, tiled=True)  41.1 us
    all_gather x1, blocking collectives, shards(): all_flux = lax.all_gather(own_flux, 'flux', axis=0, tiled=True)  39.7 us
    reduce_sum x1, other arithmetic, shards(): jnp.sum(feet.astype(jnp.float32) * coefficient[:, None, :, :, h, None], a...  18.6 us
    ppermute x5, starting transfers between devices, shards(): lax.ppermute(modeled_all, 'obs', [(dev, dev ^ hop) for dev in range(32)])  17.6 us
    ppermute x5, waiting for transfers between devices, shards(): lax.ppermute(modeled_all, 'obs', [(dev, dev ^ hop) for dev in range(32)])  16.1 us
    reduce_sum x2, other arithmetic, shards(): partial_value = jnp.sum(feet.astype(jnp.float32) * picked, axis=(1, 3, 4))  11.9 us
  transfers between devices with their start and end apart: 7, of which 6 were waited for; matrix products, arithmetic and copies ran while one was open for 15% of the time, Pallas kernels for 0%

profile of v1, /device:TPU:2, one launch (start us, length us, event | category | flops | bytes accessed | tf_op | source)
XLA Modules:
  0.0 335.5 jit_solution(2067704812837104511)
XLA Ops:
  7.2 3.4 %reshape.75 = bf16[256,32,128]{2,1,0:T(8,128)(2,1)S(1)} reshape(bf16[8,4,4,2,4096]{4,3,2,1,0:T(2,128)(2,1)} %param.7) | data formatting | bytes 4194304 | tf_op jit(solution)/shard_map/reshape | solution.py:24
  10.7 2.1 copy.126
  12.8 9.6 %all-to-all-start = ((bf16[32,256,128]{2,1,0:T(8,128)(2,1)}), bf16[32,256,128]{2,1,0:T(8,128)(2,1)S(1)}, u32[]{:S(2)}, u32[]{:S(2)}) async-start(bf16[32,256,128]{2,1,0:T(8,128)(2,1)} %copy.126), calls=%async_computation | async-start | bytes 4194304 | tf_op jit(solution)/shard_map/all_to_all | solution.py:25
  22.8 41.1 %all_gather.6 = f32[256,16]{1,0:T(8,128)S(1)} all-gather(f32[8,16]{1,0:T(8,128)S(1)} %copy.127), channel_id=1, replica_groups=mesh['flux'=16,'obs'=32] {'obs'}, dimensions={0}, use_global_device_ids=true | all-gather | bytes 16896 | tf_op jit(solution)/shard_map/all_gather | solution.py:18
  65.7 1.6 copy.130
  67.9 1.6 copy.129
  69.4 1.6 copy.139
  71.0 1.6 copy.137
  74.5 2.0 broadcast_in_dim.153
  76.5 2.6 broadcast_in_dim.154
  79.1 2.0 broadcast_in_dim.160
  81.2 3.2 broadcast_in_dim.161
  84.4 2.0 broadcast_in_dim.167
  86.4 3.2 broadcast_in_dim.168
  89.7 2.0 broadcast_in_dim.174
  91.7 3.2 broadcast_in_dim.175
  94.9 2.0 broadcast_in_dim.145
  97.0 3.2 broadcast_in_dim.146
  100.2 39.7 %all_gather.7 = bf16[512,5,128]{2,0,1:T(8,128)(2,1)} all-gather(bf16[32,5,128]{2,0,1:T(8,128)(2,1)S(1)} %constant_dynamic-slice_fusion), channel_id=1, replica_groups=mesh['flux'=16,'obs'=32] {'flux'}, dimensions={0}, use_global_device_ids=true | all-gather | bytes 696320 | tf_op jit(solution)/shard_map/all_gather | solution.py:22
  139.9 2.2 copy.131
  142.1 2.2 fusion.4
  144.5 1.1 copy.132
  145.6 1.1 copy.140
  147.9 1.1 copy.136
  149.0 1.1 copy.134
  150.2 2.2 broadcast_in_dim.157
  156.9 9.2 %multiply_reduce_fusion.5 = f32[32,256]{1,0:T(8,128)} fusion(f32[32,256,128]{2,1,0:T(8,128)S(1)} %bitcast.76, f32[32,256,128]{2,1,0:T(8,128)S(1)} %bitcast.75, f32[32,256,128]{2,1,0:T(8,128)S(1)} %bitcast.74, f32[32,256,128]{2,1,0:T(8,128)S(1)} %bitcast.73, f32[32,256,128]{2,1,0:T(8,128)S(1)} %bitcast.77, pred[32,256]{1,0:T(8,128)(4,1)S(1)} %copy-done.7, ...), kind=kLoop, calls=%fused_computation.5 | loop fusion | flops 12574720 | bytes 23142400 | tf_op jit(solution)/shard_map/reduce_sum | solution.py:41
  166.1 4.8 %reduce_sum.72 = f32[256,4,4,2]{3,2,1,0:T(4,128)} reshape(f32[32,256]{1,0:T(8,128)} %multiply_reduce_fusion.5) | data formatting | bytes 65536 | tf_op jit(solution)/shard_map/reduce_sum | solution.py:41
  170.9 2.7 reduce_sum.73
  173.6 1.9 collective-permute-start
  175.5 1.5 collective-permute-done
  178.0 3.5 %collective-permute-start.1 = (f32[256,4]{1,0:T(8,128)S(1)}, f32[256,4]{1,0:T(8,128)S(1)}, u32[]{:S(2)}, u32[]{:S(2)}) collective-permute-start(f32[256,4]{1,0:T(8,128)S(1)} %add.67), channel_id=1, source_target_pairs={{0,2},{1,3},{2,0},{3,1},{4,6},{5,7},{6,4},{7,5},{8,10},{9,11},{10,... | collective-permute-start | bytes 12296 | tf_op jit(solution)/shard_map/ppermute | solution.py:44
  181.5 3.9 %collective-permute-done.1 = f32[256,4]{1,0:T(8,128)S(1)} collective-permute-done((f32[256,4]{1,0:T(8,128)S(1)}, f32[256,4]{1,0:T(8,128)S(1)}, u32[]{:S(2)}, u32[]{:S(2)}) %collective-permute-start.1) | collective-permute-done | bytes 4128 | tf_op jit(solution)/shard_map/ppermute | solution.py:44
  185.4 4.0 %collective-permute-start.2 = (f32[256,4]{1,0:T(8,128)S(1)}, f32[256,4]{1,0:T(8,128)S(1)}, u32[]{:S(2)}, u32[]{:S(2)}) collective-permute-start(f32[256,4]{1,0:T(8,128)S(1)} %add.68), channel_id=1, source_target_pairs={{0,4},{1,5},{2,6},{3,7},{4,0},{5,1},{6,2},{7,3},{8,12},{9,13},{10,... | collective-permute-start | bytes 12296 | tf_op jit(solution)/shard_map/ppermute | solution.py:44
  189.4 4.4 %collective-permute-done.2 = f32[256,4]{1,0:T(8,128)S(1)} collective-permute-done((f32[256,4]{1,0:T(8,128)S(1)}, f32[256,4]{1,0:T(8,128)S(1)}, u32[]{:S(2)}, u32[]{:S(2)}) %collective-permute-start.2) | collective-permute-done | bytes 4128 | tf_op jit(solution)/shard_map/ppermute | solution.py:44
  193.8 3.9 %collective-permute-start.3 = (f32[256,4]{1,0:T(8,128)S(1)}, f32[256,4]{1,0:T(8,128)S(1)}, u32[]{:S(2)}, u32[]{:S(2)}) collective-permute-start(f32[256,4]{1,0:T(8,128)S(1)} %add.69), channel_id=1, source_target_pairs={{0,8},{1,9},{2,10},{3,11},{4,12},{5,13},{6,14},{7,15},{8,0},{9,1},... | collective-permute-start | bytes 12296 | tf_op jit(solution)/shard_map/ppermute | solution.py:44
  197.7 3.0 collective-permute-done.3
  201.4 4.3 %collective-permute-start.4 = (f32[256,4]{1,0:T(8,128)}, f32[256,4]{1,0:T(8,128)}, u32[]{:S(2)}, u32[]{:S(2)}) collective-permute-start(f32[256,4]{1,0:T(8,128)} %add.70), channel_id=1, source_target_pairs={{0,16},{1,17},{2,18},{3,19},{4,20},{5,21},{6,22},{7,23},{8,24},{9,... | collective-permute-start | bytes 12296 | tf_op jit(solution)/shard_map/ppermute | solution.py:44
  206.7 3.3 collective-permute-done.4
  210.0 1.8 fusion.13
  217.9 18.6 %multiply_reduce_fusion = (f32[256,4,128]{2,1,0:T(4,128)}, f32[256,4,128]{2,1,0:T(4,128)}, f32[256,4,128]{2,1,0:T(4,128)}, f32[256,4,128]{2,1,0:T(4,128)}, f32[256,4,128]{2,1,0:T(4,128)}) fusion(f32[256,4,2]{2,1,0:T(4,128)} %copy.148, f32[256,4,2]{2,1,0:T(4,128)} %copy.147, f32[256,4,2]{2,1,0:T(4,128)} %copy.146, f32[256,4,2]{2,1,0:T(4,128)} %copy.145, ...), kind=kLoop, calls=%fused_computation | loop fusion | flops 10878976 | bytes 4759552 | tf_op jit(solution)/shard_map/reduce_sum | solution.py:53
  236.5 10.5 %stack.23 = f32[256,4,5,128]{3,2,1,0:T(8,128)} concatenate(f32[256,4,1,128]{3,2,1,0:T(1,128)} %bitcast.86, f32[256,4,1,128]{3,2,1,0:T(1,128)} %bitcast.85, f32[256,4,1,128]{3,2,1,0:T(1,128)} %bitcast.84, f32[256,4,1,128]{3,2,1,0:T(1,128)} %bitcast.83, f32[256,4,1,128]{3,2,1,0:T(1,128)} %bitcast.82), dimensions={2} | concatenate | bytes 5242880 | tf_op jit(solution)/shard_map/stack | solution.py:55
  247.1 3.5 %fusion.1 = f32[512,640]{1,0:T(8,128)S(1)} fusion(f32[128,8,5,128]{3,2,1,0:T(8,128)} %bitcast.80, s32[1024]{0:T(1024)S(1)} %eq.73), kind=kOutput, calls=%fused_computation.10 | convolution fusion | flops 674234368 | bytes 3936256 | tf_op jit(solution)/shard_map/dot_general | solution.py:61
  250.5 4.4 %fusion.6 = f32[512,640]{1,0:T(8,128)} fusion(f32[512,640]{1,0:T(8,128)S(1)} %fusion.1, f32[128,8,5,128]{3,2,1,0:T(8,128)} %bitcast.81, s32[1024]{0:T(1024)S(1)} %eq.73), kind=kOutput, calls=%fused_computation.15 | convolution fusion | flops 671940608 | bytes 5246976 | tf_op jit(solution)/shard_map/dot_general | solution.py:59
  255.0 1.7 copy.149
  256.7 1.8 copy.150
  259.9 67.2 %reduce-scatter.2.cloned.1.call-done = f32[32,5,128]{2,1,0:T(8,128)} async-done(((f32[512,5,128]{2,1,0:T(8,128)}), f32[32,5,128]{2,1,0:T(8,128)}) %reduce-scatter.2.cloned.1.call-update) | async-done | bytes 81936 | tf_op jit(solution)/shard_map/reduce_scatter | solution.py:62
  327.1 1.6 copy.152
  (66 shorter events, 20.4 us)
Async XLA Ops:
  7.2 93.0 %copy-start = (bf16[32,5,4096]{2,0,1:T(8,128)(2,1)S(1)}, bf16[32,5,4096]{2,0,1:T(8,128)(2,1)}, u32[]{:S(2)}) copy-start(bf16[32,5,4096]{2,0,1:T(8,128)(2,1)} %param.11) | copy-start | bytes 3932164
  10.6 11.8 %copy-start.11 = (s32[8,4]{0,1:T(4,128)S(1)}, s32[8,4]{0,1:T(4,128)}, u32[]{:S(2)}) copy-start(s32[8,4]{0,1:T(4,128)} %param.8) | copy-start | bytes 388
  10.6 11.9 %copy-start.9 = (s32[512]{0:T(512)S(1)}, s32[512]{0:T(512)}, u32[]{:S(2)}) copy-start(s32[512]{0:T(512)} %param.10) | copy-start | bytes 6148
  10.6 11.9 %copy-start.10 = (s32[8,4]{0,1:T(4,128)S(1)}, s32[8,4]{0,1:T(4,128)}, u32[]{:S(2)}) copy-start(s32[8,4]{0,1:T(4,128)} %param.9) | copy-start | bytes 388
  10.7 12.1 %copy-start.12 = (f32[8,4]{0,1:T(4,128)S(1)}, f32[8,4]{0,1:T(4,128)}, u32[]{:S(2)}) copy-start(f32[8,4]{0,1:T(4,128)} %param.13) | copy-start | bytes 388
  10.7 12.1 %copy-start.13 = (f32[8,4]{0,1:T(4,128)S(1)}, f32[8,4]{0,1:T(4,128)}, u32[]{:S(2)}) copy-start(f32[8,4]{0,1:T(4,128)} %param.12) | copy-start | bytes 388
  12.8 137.4 %all-to-all-start = ((bf16[32,256,128]{2,1,0:T(8,128)(2,1)}), bf16[32,256,128]{2,1,0:T(8,128)(2,1)S(1)}, u32[]{:S(2)}, u32[]{:S(2)}) async-start(bf16[32,256,128]{2,1,0:T(8,128)(2,1)} %copy.126), calls=%async_computation | async-start | bytes 4194304 | tf_op jit(solution)/shard_map/all_to_all | solution.py:25
  22.4 304.7 %reduce-scatter.2.cloned.1.call-start = ((), (), s32[]{:S(2)}) async-start(), calls=%async_computation.2 | async-start | bytes 2228224 | tf_op jit(solution)/shard_map/reduce_scatter | solution.py:62
  150.2 2.2 copy-start.4
  150.2 3.3 copy-start.3
  152.4 2.2 copy-start.2
  153.5 2.2 copy-start.1
  154.6 2.2 copy-start.5
  154.6 2.2 copy-start.6
  154.7 2.2 copy-start.7
  154.7 2.2 copy-start.8
  173.6 3.4 %collective-permute-start = (f32[256,4]{1,0:T(8,128)}, f32[256,4]{1,0:T(8,128)S(1)}, u32[]{:S(2)}, u32[]{:S(2)}) collective-permute-start(f32[256,4]{1,0:T(8,128)} %reduce_sum.73), channel_id=1, source_target_pairs={{0,1},{1,0},{2,3},{3,2},{4,5},{5,4},{6,7},{7,6},{8,9},{9,8},{10,11... | collective-permute-start | bytes 12296 | tf_op jit(solution)/shard_map/ppermute | solution.py:44
  178.0 7.4 %collective-permute-start.1 = (f32[256,4]{1,0:T(8,128)S(1)}, f32[256,4]{1,0:T(8,128)S(1)}, u32[]{:S(2)}, u32[]{:S(2)}) collective-permute-start(f32[256,4]{1,0:T(8,128)S(1)} %add.67), channel_id=1, source_target_pairs={{0,2},{1,3},{2,0},{3,1},{4,6},{5,7},{6,4},{7,5},{8,10},{9,11},{10,... | collective-permute-start | bytes 12296 | tf_op jit(solution)/shard_map/ppermute | solution.py:44
  185.4 8.4 %collective-permute-start.2 = (f32[256,4]{1,0:T(8,128)S(1)}, f32[256,4]{1,0:T(8,128)S(1)}, u32[]{:S(2)}, u32[]{:S(2)}) collective-permute-start(f32[256,4]{1,0:T(8,128)S(1)} %add.68), channel_id=1, source_target_pairs={{0,4},{1,5},{2,6},{3,7},{4,0},{5,1},{6,2},{7,3},{8,12},{9,13},{10,... | collective-permute-start | bytes 12296 | tf_op jit(solution)/shard_map/ppermute | solution.py:44
  193.8 6.9 %collective-permute-start.3 = (f32[256,4]{1,0:T(8,128)S(1)}, f32[256,4]{1,0:T(8,128)S(1)}, u32[]{:S(2)}, u32[]{:S(2)}) collective-permute-start(f32[256,4]{1,0:T(8,128)S(1)} %add.69), channel_id=1, source_target_pairs={{0,8},{1,9},{2,10},{3,11},{4,12},{5,13},{6,14},{7,15},{8,0},{9,1},... | collective-permute-start | bytes 12296 | tf_op jit(solution)/shard_map/ppermute | solution.py:44
  201.4 8.7 %collective-permute-start.4 = (f32[256,4]{1,0:T(8,128)}, f32[256,4]{1,0:T(8,128)}, u32[]{:S(2)}, u32[]{:S(2)}) collective-permute-start(f32[256,4]{1,0:T(8,128)} %add.70), channel_id=1, source_target_pairs={{0,16},{1,17},{2,18},{3,19},{4,20},{5,21},{6,22},{7,23},{8,24},{9,... | collective-permute-start | bytes 12296 | tf_op jit(solution)/shard_map/ppermute | solution.py:44
Sparse Core Ops, SparseCore 0:
  258.7 68.4 reduce-scatter.1
